TPU v7x, 32 devices: a whole 2x2x4 slice. The times are simulated.
32 devices in a mesh: row: 8 (over y, x, core), col: 4 (over z).
Axes of the slice: x: 2, y: 2, z: 4, core: 2. Of those that a mesh axis runs over, the one named last changes fastest.
Arguments:
- features: float32 [4096, 128], P(('row', 'col')), may hold values from -6 to 6
- weight: float32 [128, 128], replicated, may hold values from -0.5 to 0.5
- layer_bias: float32 [128], replicated, may hold values from -3 to 3
- degree_scale: float32 [4096], P(('row', 'col')), may hold values from 0.05 to 0.5
- tile_values: bfloat16 [8, 4, 32, 128, 128], P('row', 'col'), may hold values from 0 to 1
- tile_slots: int32 [8, 4, 32], P('row', 'col'), may hold values from 0 to 31, as said below
- tile_count: int32 [8, 4], P('row', 'col'), may hold values from 1 to 32, as said below
- cotangent: float32 [4096, 128], P(('row', 'col')), may hold values from -6 to 6
Outputs:
- activations: float32 [4096, 128], P(('row', 'col'))
- feature_grad: float32 [4096, 128], P(('row', 'col'))
- weight_grad: float32 [128, 128], replicated
- bias_grad: float32 [128], replicated
Inputs may be any that keep to these rules, and one draw needn't show every extreme that they name: `tile_slots`: the first tile_count[r, c] slots of a device name distinct positions of its grid of 8 by 4 tiles (row u, column v as p = u * 4 + v); later slots hold other positions in range and are ignored. `tile_count`: counts are skewed across devices; in every draw some device has a full list of 32 tiles.
All inputs are finite; a program needn't handle non-finite values.
Results may differ from a plain program's by a relative error of at most 0.0059.
Values may be sent and summed in bfloat16 or wider, within the bound.
A program may use at most 64 MiB of HBM per device.

v0:
```python
import math
import jax
import jax.numpy as jnp
from jax import lax
from jax.sharding import PartitionSpec as P

TBLK = 32


def gelu_pair(values):
    argument = 0.7978845608028654 * (values + 0.044715 * values * values * values)
    tangent = jnp.tanh(argument)
    output = 0.5 * values * (1.0 + tangent)
    slopes = 0.5 * (1.0 + tangent) + 0.5 * values * (
        1.0 - tangent * tangent
    ) * 0.7978845608028654 * (1.0 + 3.0 * 0.044715 * values * values)
    return (output, slopes)


def aggregate(
    blocks, target_index, source_index, live_count, source, target_first, target_blocks, form
):
    tile_size = blocks.shape[1]
    feature_width = source.shape[1]
    source_blocks = source.reshape(-1, tile_size, feature_width)
    block_count = (live_count + TBLK - 1) // TBLK
    positions = target_first + jnp.arange(target_blocks, dtype=jnp.int32)

    def accumulate(block_index, totals):
        first_tile = block_index * TBLK
        tile_block = lax.dynamic_slice_in_dim(blocks, first_tile, TBLK, 0)
        targets = lax.dynamic_slice_in_dim(target_index, first_tile, TBLK, 0)
        sources = lax.dynamic_slice_in_dim(source_index, first_tile, TBLK, 0)
        picked = source_blocks[sources]
        products = jnp.einsum(form, tile_block, picked, preferred_element_type=jnp.float32)
        live_mask = first_tile + jnp.arange(TBLK, dtype=jnp.int32) < live_count
        selector = ((targets[None, :] == positions[:, None]) & live_mask[None, :]).astype(
            jnp.float32
        )
        return totals + jnp.dot(
            selector,
            products.reshape(TBLK, tile_size * feature_width),
            precision=lax.Precision.HIGHEST,
            preferred_element_type=jnp.float32,
        )

    empty = jnp.zeros((target_blocks, tile_size * feature_width), jnp.float32)
    totals = lax.fori_loop(0, block_count, accumulate, empty)
    return totals.reshape(target_blocks * tile_size, feature_width)


def local(
    features, weight, layer_bias, degree_scale, tile_values, tile_slots, tile_count, cotangent
):
    highest = lax.Precision.HIGHEST
    own_rows = features.shape[0]
    tile_size = tile_values.shape[3]
    row_devices = lax.axis_size("row")
    col_devices = lax.axis_size("col")
    local_blocks = own_rows // tile_size
    column_blocks = col_devices * local_blocks
    row_blocks = row_devices * local_blocks
    blocks = tile_values[0, 0]
    slots = tile_slots[0, 0]
    live_count = tile_count[0, 0]
    local_rows = slots // column_blocks
    local_cols = slots % column_blocks
    norm_factor = 1.0 / math.sqrt(own_rows * row_devices * col_devices)
    projected = jnp.dot(features, weight, precision=highest, preferred_element_type=jnp.float32)
    scaled = (degree_scale[:, None] * projected).astype(jnp.bfloat16)
    gathered = lax.all_gather(scaled, "col", axis=0, tiled=True)
    partial_value = aggregate(
        blocks,
        local_rows,
        local_cols,
        live_count,
        gathered,
        0 // tile_size,
        row_blocks * tile_size // tile_size,
        "tij,tjf->tif",
    )
    summed = lax.psum_scatter(partial_value, "row", scatter_dimension=0, tiled=True)
    preact = degree_scale[:, None] * summed + layer_bias[None, :]
    activation, slopes = gelu_pair(preact)
    delta = cotangent * slopes
    bias_part = jnp.sum(delta, axis=0)
    delta_scaled = (degree_scale[:, None] * delta).astype(jnp.bfloat16)
    delta_rows = lax.all_gather(delta_scaled, "row", axis=0, tiled=True)
    back_partial = aggregate(
        blocks,
        local_cols,
        local_rows,
        live_count,
        delta_rows,
        0 // tile_size,
        column_blocks * tile_size // tile_size,
        "tji,tjf->tif",
    )
    back_summed = lax.psum_scatter(back_partial, "col", scatter_dimension=0, tiled=True)
    scaled_grad = degree_scale[:, None] * back_summed
    weight_part = jnp.dot(
        features.T, scaled_grad, precision=highest, preferred_element_type=jnp.float32
    )
    weight_total, bias_total = lax.psum((weight_part, bias_part), ("row", "col"))
    feature_grad = jnp.dot(
        scaled_grad, weight.T, precision=highest, preferred_element_type=jnp.float32
    )
    return (activation, feature_grad, weight_total * norm_factor, bias_total * norm_factor)


def solution(mesh):
    return jax.shard_map(
        local,
        mesh=mesh,
        in_specs=(
            P(("row", "col"), None),
            P(),
            P(),
            P(("row", "col")),
            P("row", "col", None, None, None),
            P("row", "col", None),
            P("row", "col"),
            P(("row", "col"), None),
        ),
        out_specs=(P(("row", "col"), None), P(("row", "col"), None), P(), P()),
        check_vma=False,
    )
```

profile of v0, /device:TPU:1, one launch (start us, length us, event | category | flops | bytes accessed | tf_op | source)
XLA Modules:
  0.0 262.1 jit_solution(9816274243464607919)
XLA Ops:
  8.6 1.0 fusion.18
  9.6 12.1 %all_gather.6 = bf16[512,128]{1,0:T(8,128)(2,1)S(1)} all-gather(bf16[128,128]{1,0:T(8,128)(2,1)S(1)} %fusion.18), channel_id=1, replica_groups=mesh['row'=8,'col'=4] {'col'}, dimensions={0}, use_global_device_ids=true | all-gather | bytes 163840 | tf_op jit(solution)/shard_map/all_gather | solution.py:71
  21.8 8.1 %while.22 = (s32[]{:T(128)}, f32[8,16384]{1,0:T(8,128)S(1)}, s32[]{:T(128)}, s32[32]{0:T(128)S(1)}, s32[]{:T(128)}, /*index=5*/s32[32]{0:T(128)S(1)}, bf16[4,128...) while((s32[]{:T(128)}, f32[8,16384]{1,0:T(8,128)S(1)}, s32[]{:T(128)}, ...), condition=%wide.region_1.2_spmd.clone, body=%wide.region_0.1_spmd.clone.sunk | while | flops 184682144 | bytes 17830740 | solution.py:48
  21.8 0.7 gather_fusion
  23.0 2.2 convolution_bitcast_fusion.5
  25.3 1.9 copy.37
  27.8 2.0 convolution_add_fusion.4
  29.9 0.9 reshape.69
  30.8 37.4 %reduce-scatter.3.cloned.1.call-done = f32[128,128]{1,0:T(8,128)} async-done(((f32[1024,128]{1,0:T(8,128)}), f32[128,128]{1,0:T(8,128)}) %reduce-scatter.3.cloned.1.call-update) | async-done | bytes 65552 | tf_op jit(solution)/shard_map/reduce_scatter | solution.py:82
  68.2 1.6 fusion.30
  69.9 10.3 %all_gather.7 = bf16[1024,128]{1,0:T(8,128)(2,1)S(1)} all-gather(bf16[128,128]{1,0:T(8,128)(2,1)S(1)} %multiply_convert_fusion), channel_id=1, replica_groups=mesh['row'=8,'col'=4] {'row'}, dimensions={0}, use_global_device_ids=true | all-gather | bytes 294912 | tf_op jit(solution)/shard_map/all_gather | solution.py:88
  80.2 0.7 broadcast_in_dim.5
  80.9 8.9 %while.23 = (s32[]{:T(128)}, f32[4,16384]{1,0:T(4,128)}, s32[]{:T(128)}, s32[32]{0:T(128)S(1)}, s32[]{:T(128)}, /*index=5*/s32[32]{0:T(128)S(1)}, bf16[8,128,128...) while((s32[]{:T(128)}, f32[4,16384]{1,0:T(4,128)}, s32[]{:T(128)}, ...), condition=%wide.region_4.5_spmd.clone, body=%wide.region_3.4_spmd.clone.sunk | while | flops 159450528 | bytes 13112121 | solution.py:48
  81.0 0.7 gather_fusion.1
  81.7 1.9 convolution_bitcast_fusion.6
  83.6 1.9 copy.39
  86.2 3.6 %convolution_add_fusion.5 = f32[4,16384]{1,0:T(4,128)} fusion(f32[4,16384]{1,0:T(4,128)} %get-tuple-element.326, f32[4,8,128,128]{3,2,1,0:T(8,128)S(1)} %bitcast.80, s32[32]{0:T(128)S(1)} %get-tuple-element.338, pred[32]{0:T(512)(128)(4,1)S(1)} %add_compare_fusion.5), kind=kOutput, calls=%fused_computation.16.clone.1 | convolution fusion | flops 25231616 | bytes 2621600 | tf_op jit(solution)/shard_map/while/body/dot_general | solution.py:40
  89.8 1.8 reshape.71
  91.7 38.0 %psum.15 = f32[128]{0:T(128)S(1)} all-reduce(f32[128]{0:T(128)S(1)} %get-tuple-element.180), channel_id=1, replica_groups=mesh['row'=8,'col'=4] {'row','col'}, use_global_device_ids=true, to_apply=%region_8.9 | all-reduce | flops 128 | bytes 1024 | tf_op jit(solution)/shard_map/psum | solution.py:104
  130.2 1.8 convolution_bitcast_fusion.2
  132.0 1.8 fusion.26
  133.8 120.2 %all-reduce.2.cloned.1.call-done = f32[128,128]{0,1:T(8,128)} async-done(((f32[128,128]{0,1:T(8,128)}), f32[128,128]{0,1:T(8,128)}) %all-reduce.2.cloned.1.call-update) | async-done | bytes 65552 | tf_op jit(solution)/shard_map/psum | solution.py:104
  254.0 0.8 broadcast_multiply_fusion
  254.8 0.7 copy.19
  (31 shorter events, 3.3 us)
Async XLA Ops:
  7.2 1.4 copy-start
  7.2 61.0 %reduce-scatter.3.cloned.1.call-start = ((), (), s32[]{:S(2)}) async-start(), calls=%async_computation.2 | async-start | bytes 589824 | tf_op jit(solution)/shard_map/reduce_scatter | solution.py:82
  21.7 46.4 %copy-start.4 = (f32[128,128]{1,0:T(8,128)S(1)}, f32[128,128]{1,0:T(8,128)}, u32[]{:S(2)}) copy-start(f32[128,128]{1,0:T(8,128)} %param.19) | copy-start | bytes 196612
  21.8 46.4 %copy-start.5 = (f32[128]{0:T(128)S(1)}, f32[128]{0:T(128)}, u32[]{:S(2)}) copy-start(f32[128]{0:T(128)} %param.15) | copy-start | bytes 1540
  21.8 46.4 %copy-start.6 = (f32[128]{0:T(128)S(1)}, f32[128]{0:T(128)}, u32[]{:S(2)}) copy-start(f32[128]{0:T(128)} %param.14) | copy-start | bytes 1540
  21.8 1.2 copy-start.1
  29.9 51.1 %copy-start.2 = (bf16[32,128,128]{2,1,0:T(8,128)(2,1)S(1)}, bf16[32,128,128]{2,1,0:T(8,128)(2,1)}, u32[]{:S(2)}) copy-start(bf16[32,128,128]{2,1,0:T(8,128)(2,1)} %get-tuple-element.348) | copy-start | bytes 3145732
  30.8 99.4 %reduce-scatter.5.cloned.1.call-start = ((), (), s32[]{:S(2)}) async-start(), calls=%async_computation.3 | async-start | bytes 327680 | tf_op jit(solution)/shard_map/reduce_scatter | solution.py:99
  80.9 51.1 %copy-start.3 = (f32[128,128]{1,0:T(8,128)S(1)}, f32[128,128]{1,0:T(8,128)}, u32[]{:S(2)}) copy-start(f32[128,128]{1,0:T(8,128)} %param.13) | copy-start | bytes 196612
  91.6 162.4 %all-reduce.2.cloned.1.call-start = ((), (), s32[]{:S(2)}) async-start(), calls=%async_computation.4 | async-start | bytes 131072 | tf_op jit(solution)/shard_map/psum | solution.py:104
Sparse Core Ops, SparseCore 0:
  30.9 37.2 reduce-scatter.2
  91.8 17.0 reduce-scatter.4
  132.1 121.7 all-reduce.1
where the time goes:
time: 263 us; the launch traced here: 262 us
  waiting for transfers between devices  158 us (60%)
  blocking collectives  60.4 us (23%)
  between operations  14.5 us (6%)
  matrix products  14.3 us (5%)
  local copies, waits for them, and re-layouts  10 us (4%)
  other arithmetic  5.02 us (2%)
    psum x1, waiting for transfers between devices, local(): lax.psum((weight_part, bias_part), ('row', 'col'))  120 us
    psum x1, blocking collectives, local(): lax.psum((weight_part, bias_part), ('row', 'col'))  38 us
    reduce_scatter x1, waiting for transfers between devices, local(): lax.psum_scatter(partial_value, 'row', scatter_dimension=0, tiled=True)  37.4 us
    all_gather x1, blocking collectives, local(): gathered = lax.all_gather(scaled, 'col', axis=0, tiled=True)  12.1 us
    all_gather x1, blocking collectives, local(): delta_rows = lax.all_gather(delta_scaled, 'row', axis=0, tiled=True)  10.3 us
    dot_general x2, matrix products, accumulate(): jnp.dot(selector, products.reshape(TBLK, tile_size * feature_width), prec...  5.6 us
  transfers between devices with their start and end apart: 3, of which 2 were waited for; matrix products, arithmetic and copies ran while one was open for 1% of the time, Pallas kernels for 0%

commit v1 on v0

--- a/solution.py
+++ b/solution.py
@@ -101,7 +101,7 @@
     weight_part = jnp.dot(
         features.T, scaled_grad, precision=highest, preferred_element_type=jnp.float32
     )
-    weight_total, bias_total = lax.psum((weight_part, bias_part), ("row", "col"))
+    weight_total, bias_total = lax.psum(lax.psum((weight_part, bias_part), "col"), "row")
     feature_grad = jnp.dot(
         scaled_grad, weight.T, precision=highest, preferred_element_type=jnp.float32
     )

time: 263 us -> 213 us (0.81)
  waiting for transfers between devices: 158 us -> 120 us
  blocking collectives: 60.4 us -> 45.9 us
    psum x1 -> x2, waiting for transfers between devices: 120 us -> 82.9 us  [the longest x1 55.3 us: local(): lax.psum(lax.psum((weight_part, bias_part), 'col'), 'row')]
    psum x1 -> x2, blocking collectives: 38 us -> 23.5 us  [the longest x1 13.8 us: local(): lax.psum(lax.psum((weight_part, bias_part), 'col'), 'row')]
  transfers between devices with their start and end apart: 3 -> 4, of which waited for: 2 -> 3; matrix products, arithmetic and copies ran while one was open for 1% -> 1% of each run, Pallas kernels for 0% -> 0%
where the time goes in v1:
time: 213 us; the launch traced here: 210 us
  waiting for transfers between devices  120 us (56%)
  blocking collectives  45.9 us (22%)
  between operations  14.5 us (7%)
  matrix products  14.3 us (7%)
  local copies, waits for them, and re-layouts  10 us (5%)
  other arithmetic  5.02 us (2%)
    psum x1, waiting for transfers between devices, local(): lax.psum(lax.psum((weight_part, bias_part), 'col'), 'row')  55.3 us
    reduce_scatter x1, waiting for transfers between devices, local(): lax.psum_scatter(partial_value, 'row', scatter_dimension=0, tiled=True)  37.4 us
    psum x1, waiting for transfers between devices, local(): lax.psum((weight_part, bias_part), 'col')  27.6 us
    psum x1, blocking collectives, local(): lax.psum(lax.psum((weight_part, bias_part), 'col'), 'row')  13.8 us
    all_gather x1, blocking collectives, local(): gathered = lax.all_gather(scaled, 'col', axis=0, tiled=True)  12.1 us
    all_gather x1, blocking collectives, local(): delta_rows = lax.all_gather(delta_scaled, 'row', axis=0, tiled=True)  10.3 us
    psum x1, blocking collectives, local(): lax.psum((weight_part, bias_part), 'col')  9.68 us
    dot_general x2, matrix products, accumulate(): jnp.dot(selector, products.reshape(TBLK, tile_size * feature_width), prec...  5.62 us
  transfers between devices with their start and end apart: 4, of which 3 were waited for; matrix products, arithmetic and copies ran while one was open for 1% of the time, Pallas kernels for 0%

profile of v1, /device:TPU:1, one launch (start us, length us, event | category | flops | bytes accessed | tf_op | source)
XLA Modules:
  0.0 210.4 jit_solution(3515346471663710258)
XLA Ops:
  8.6 1.0 fusion.18
  9.6 12.1 %all_gather.6 = bf16[512,128]{1,0:T(8,128)(2,1)S(1)} all-gather(bf16[128,128]{1,0:T(8,128)(2,1)S(1)} %fusion.18), channel_id=1, replica_groups=mesh['row'=8,'col'=4] {'col'}, dimensions={0}, use_global_device_ids=true | all-gather | bytes 163840 | tf_op jit(solution)/shard_map/all_gather | solution.py:71
  21.8 8.1 %while.22 = (s32[]{:T(128)}, f32[8,16384]{1,0:T(8,128)S(1)}, s32[]{:T(128)}, s32[32]{0:T(128)S(1)}, s32[]{:T(128)}, /*index=5*/s32[32]{0:T(128)S(1)}, bf16[4,128...) while((s32[]{:T(128)}, f32[8,16384]{1,0:T(8,128)S(1)}, s32[]{:T(128)}, ...), condition=%wide.region_1.2_spmd.clone, body=%wide.region_0.1_spmd.clone.sunk | while | flops 184682144 | bytes 17830740 | solution.py:48
  21.8 0.7 gather_fusion
  23.0 2.2 %convolution_bitcast_fusion.5 = f32[32,128,128]{1,2,0:T(8,128)} fusion(bf16[32,128,128]{2,1,0:T(8,128)(2,1)S(1)} %gather_fusion, bf16[32,128,128]{2,1,0:T(8,128)(2,1)S(1)} %copy-done.1), kind=kOutput, calls=%fused_computation.7.clone.1 | convolution fusion | flops 134217728 | bytes 4194304 | tf_op jit(solution)/shard_map/while/body/tij,tjf->tif/dot_general | solution.py:35
  25.3 1.9 copy.37
  27.8 2.0 convolution_add_fusion.4
  29.9 0.9 reshape.69
  30.8 37.4 %reduce-scatter.3.cloned.1.call-done = f32[128,128]{1,0:T(8,128)} async-done(((f32[1024,128]{1,0:T(8,128)}), f32[128,128]{1,0:T(8,128)}) %reduce-scatter.3.cloned.1.call-update) | async-done | bytes 65552 | tf_op jit(solution)/shard_map/reduce_scatter | solution.py:82
  68.2 1.6 fusion.30
  69.9 10.3 %all_gather.7 = bf16[1024,128]{1,0:T(8,128)(2,1)S(1)} all-gather(bf16[128,128]{1,0:T(8,128)(2,1)S(1)} %multiply_convert_fusion), channel_id=1, replica_groups=mesh['row'=8,'col'=4] {'row'}, dimensions={0}, use_global_device_ids=true | all-gather | bytes 294912 | tf_op jit(solution)/shard_map/all_gather | solution.py:88
  80.2 0.8 broadcast_in_dim.5
  80.9 8.9 %while.23 = (s32[]{:T(128)}, f32[4,16384]{1,0:T(4,128)}, s32[]{:T(128)}, s32[32]{0:T(128)S(1)}, s32[]{:T(128)}, /*index=5*/s32[32]{0:T(128)S(1)}, bf16[8,128,128...) while((s32[]{:T(128)}, f32[4,16384]{1,0:T(4,128)}, s32[]{:T(128)}, ...), condition=%wide.region_4.5_spmd.clone, body=%wide.region_3.4_spmd.clone.sunk | while | flops 159450528 | bytes 13112121 | solution.py:48
  81.7 1.9 convolution_bitcast_fusion.6
  83.6 1.9 copy.39
  86.2 3.6 %convolution_add_fusion.5 = f32[4,16384]{1,0:T(4,128)} fusion(f32[4,16384]{1,0:T(4,128)} %get-tuple-element.326, f32[4,8,128,128]{3,2,1,0:T(8,128)S(1)} %bitcast.80, s32[32]{0:T(128)S(1)} %get-tuple-element.338, pred[32]{0:T(512)(128)(4,1)S(1)} %add_compare_fusion.5), kind=kOutput, calls=%fused_computation.16.clone.1 | convolution fusion | flops 25231616 | bytes 2621600 | tf_op jit(solution)/shard_map/while/body/dot_general | solution.py:40
  89.8 1.8 reshape.71
  91.7 9.7 %psum.30 = f32[128]{0:T(128)S(1)} all-reduce(f32[128]{0:T(128)S(1)} %get-tuple-element.180), channel_id=1, replica_groups=mesh['row'=8,'col'=4] {'col'}, use_global_device_ids=true, to_apply=%region_9.10 | all-reduce | flops 128 | bytes 1024 | tf_op jit(solution)/shard_map/psum | solution.py:104
  101.4 13.8 %psum.31 = f32[128]{0:T(128)S(1)} all-reduce(f32[128]{0:T(128)S(1)} %psum.30), channel_id=1, replica_groups=mesh['row'=8,'col'=4] {'row'}, use_global_device_ids=true, to_apply=%region_10.11 | all-reduce | flops 128 | bytes 1024 | tf_op jit(solution)/shard_map/psum | solution.py:104
  115.2 1.8 convolution_bitcast_fusion.2
  117.6 27.6 %all-reduce.3.cloned.1.call-done = f32[128,128]{0,1:T(8,128)} async-done(((f32[128,128]{0,1:T(8,128)}), f32[128,128]{0,1:T(8,128)}) %all-reduce.3.cloned.1.call-update) | async-done | bytes 65552 | tf_op jit(solution)/shard_map/psum | solution.py:104
  145.3 1.8 fusion.26
  147.1 55.3 %all-reduce.5.cloned.1.call-done = f32[128,128]{0,1:T(8,128)} async-done(((f32[128,128]{0,1:T(8,128)}), f32[128,128]{0,1:T(8,128)}) %all-reduce.5.cloned.1.call-update) | async-done | bytes 65552 | tf_op jit(solution)/shard_map/psum | solution.py:104
  202.3 0.8 broadcast_multiply_fusion
  (35 shorter events, 4.8 us)
Async XLA Ops:
  7.2 1.4 copy-start
  7.2 61.0 %reduce-scatter.3.cloned.1.call-start = ((), (), s32[]{:S(2)}) async-start(), calls=%async_computation.2 | async-start | bytes 589824 | tf_op jit(solution)/shard_map/reduce_scatter | solution.py:82
  21.7 46.4 %copy-start.4 = (f32[128,128]{1,0:T(8,128)S(1)}, f32[128,128]{1,0:T(8,128)}, u32[]{:S(2)}) copy-start(f32[128,128]{1,0:T(8,128)} %param.19) | copy-start | bytes 196612
  21.8 46.4 %copy-start.5 = (f32[128]{0:T(128)S(1)}, f32[128]{0:T(128)}, u32[]{:S(2)}) copy-start(f32[128]{0:T(128)} %param.15) | copy-start | bytes 1540
  21.8 46.4 %copy-start.6 = (f32[128]{0:T(128)S(1)}, f32[128]{0:T(128)}, u32[]{:S(2)}) copy-start(f32[128]{0:T(128)} %param.14) | copy-start | bytes 1540
  21.8 1.2 copy-start.1
  29.8 51.1 %copy-start.2 = (bf16[32,128,128]{2,1,0:T(8,128)(2,1)S(1)}, bf16[32,128,128]{2,1,0:T(8,128)(2,1)}, u32[]{:S(2)}) copy-start(bf16[32,128,128]{2,1,0:T(8,128)(2,1)} %get-tuple-element.349) | copy-start | bytes 3145732
  30.8 84.5 %reduce-scatter.5.cloned.1.call-start = ((), (), s32[]{:S(2)}) async-start(), calls=%async_computation.3 | async-start | bytes 327680 | tf_op jit(solution)/shard_map/reduce_scatter | solution.py:99
  80.9 64.3 %copy-start.3 = (f32[128,128]{1,0:T(8,128)S(1)}, f32[128,128]{1,0:T(8,128)}, u32[]{:S(2)}) copy-start(f32[128,128]{1,0:T(8,128)} %param.13) | copy-start | bytes 196612
  91.7 53.6 %all-reduce.3.cloned.1.call-start = ((), (), s32[]{:S(2)}) async-start(), calls=%async_computation.4 | async-start | bytes 131072 | tf_op jit(solution)/shard_map/psum | solution.py:104
  117.1 85.3 %all-reduce.5.cloned.1.call-start = ((), (), s32[]{:S(2)}) async-start(), calls=%async_computation.5 | async-start | bytes 131072 | tf_op jit(solution)/shard_map/psum | solution.py:104
Sparse Core Ops, SparseCore 0:
  30.9 37.2 reduce-scatter.2
  91.8 17.1 reduce-scatter.4
  117.2 28.0 all-reduce.2
  148.2 54.1 all-reduce.4
